TPU v7x, 256 devices: a whole 4x4x8 slice. The times are simulated.
256 devices in a mesh: head: 8 (over y, core), ctx: 32 (over z, x).
Axes of the slice: x: 4, y: 4, z: 8, core: 2. Of those that a mesh axis runs over, the one named last changes fastest.
Arguments:
- query_matrix: bfloat16 [32768, 4096], P(('ctx', 'head')), may hold values from -6 to 6
- key_matrix: bfloat16 [32768, 2048], P(('ctx', 'head')), may hold values from -6 to 6
- value_matrix: bfloat16 [32768, 2048], P(('ctx', 'head')), may hold values from -6 to 6
- documents: int32 [32768], replicated, may hold values from 0 to 46, as said below
- readers: int32 [32, 4], replicated, may hold values from 0 to 1, as said below
Outputs:
- attended: bfloat16 [32768, 4096], P(('ctx', 'head'))
Inputs may be any that keep to these rules, and one draw needn't show every extreme that they name: `documents`: starts at 0 and never falls from one token to the next; it rises by one exactly twice inside every key block other than key blocks 0 to 3 and 12 to 16, and nowhere else. `readers`: every entry of column 0 is 1. Row 0 and rows 12 to 16 are all 1.
All inputs are finite; a program needn't handle non-finite values.
Results may differ from a plain program's by a relative error of at most 0.0038.
Values may be sent and summed in bfloat16 or wider, within the bound.
A program may use at most 192 MiB of HBM per device.

v0:
```python
import jax
import jax.numpy as jnp
from jax import lax
from jax.sharding import PartitionSpec as P

QUERY_HEADS = 32
KEY_VALUE_HEADS = 16
HEAD_WIDTH = 128
score_scale = 168.0 ** (-0.5)
neg_large = -1e30


def passed_along(value, axis, steps):
    count = lax.axis_size(axis)
    leading, last = (max(0, -steps), min(count, count - steps))
    return lax.ppermute(value, axis, [(source, source + steps) for source in range(leading, last)])


def attend_block(running, grouped, block, query_docs, query_pos, key_docs, key_pos, allowed):
    maxima, totals, accumulated = running
    heads_local = block.shape[1] // (2 * HEAD_WIDTH)
    key_part = block[:, : heads_local * HEAD_WIDTH].reshape(block.shape[0], heads_local, HEAD_WIDTH)
    value_part = block[:, heads_local * HEAD_WIDTH :].reshape(
        block.shape[0], heads_local, HEAD_WIDTH
    )
    scores = (
        jnp.einsum("qgmd,kgd->qgmk", grouped, key_part, preferred_element_type=jnp.float32)
        * score_scale
    )
    visible = (
        (query_docs[:, None] == key_docs[None, :])
        & (key_pos[None, :] <= query_pos[:, None])
        & allowed
    )
    visible = visible[:, None, None, :]
    scores = jnp.where(visible, scores, neg_large)
    new_max = jnp.maximum(maxima, jnp.max(scores, axis=3))
    weights = jnp.where(visible, jnp.exp(scores - new_max[..., None]), 0.0)
    rescale = jnp.exp(maxima - new_max)
    totals = totals * rescale + jnp.sum(weights, axis=3)
    product = jnp.einsum(
        "qgmk,kgd->qgmd",
        weights.astype(jnp.bfloat16),
        value_part,
        preferred_element_type=jnp.float32,
    )
    accumulated = accumulated * rescale[..., None] + product
    return (new_max, totals, accumulated)


def per_device(query_matrix, key_matrix, value_matrix, documents, readers):
    query_local, key_local, value_local = (
        lax.all_to_all(query_matrix, "head", split_axis=1, concat_axis=0, tiled=True),
        lax.all_to_all(key_matrix, "head", split_axis=1, concat_axis=0, tiled=True),
        lax.all_to_all(value_matrix, "head", split_axis=1, concat_axis=0, tiled=True),
    )
    rows_per_block = query_local.shape[0]
    heads_local = key_local.shape[1] // HEAD_WIDTH
    query_group_width = QUERY_HEADS // KEY_VALUE_HEADS
    window = readers.shape[1]
    shard_index = lax.axis_index("ctx")
    stacked = jnp.concatenate([key_local, value_local], axis=1)
    block_list = [stacked] + [
        passed_along(stacked, "ctx", distance) for distance in range(1, window)
    ]
    query_start = shard_index * rows_per_block
    row_iota = jnp.arange(rows_per_block, dtype=jnp.int32)
    query_pos = query_start + row_iota
    query_docs = lax.dynamic_slice_in_dim(documents, query_start, rows_per_block)
    grouped = query_local.reshape(rows_per_block, heads_local, query_group_width, HEAD_WIDTH)
    running = (
        jnp.full((rows_per_block, heads_local, query_group_width), neg_large, jnp.float32),
        jnp.zeros((rows_per_block, heads_local, query_group_width), jnp.float32),
        jnp.zeros((rows_per_block, heads_local, query_group_width, HEAD_WIDTH), jnp.float32),
    )
    for distance in range(window):
        owner_block = shard_index - distance
        safe_owner = jnp.maximum(owner_block, 0)
        key_pos = owner_block * rows_per_block + row_iota
        key_docs = lax.dynamic_slice_in_dim(documents, safe_owner * rows_per_block, rows_per_block)
        allowed = (owner_block >= 0) & (readers[safe_owner, distance] > 0)
        running = attend_block(
            running,
            grouped,
            block_list[distance],
            query_docs,
            query_pos,
            key_docs,
            key_pos,
            allowed,
        )
    maxima, totals, accumulated = running
    outputs = (
        (accumulated / totals[..., None])
        .astype(jnp.bfloat16)
        .reshape(rows_per_block, heads_local * query_group_width * HEAD_WIDTH)
    )
    return lax.all_to_all(outputs, "head", split_axis=0, concat_axis=1, tiled=True)


def solution(mesh):
    placed = (
        P(("ctx", "head"), None),
        P(("ctx", "head"), None),
        P(("ctx", "head"), None),
        P(),
        P(),
    )
    return jax.shard_map(
        per_device, mesh=mesh, in_specs=placed, out_specs=P(("ctx", "head"), None), check_vma=False
    )
```

profile of v0, /device:TPU:128, one launch (start us, length us, event | category | flops | bytes accessed | tf_op | source)
XLA Modules:
  0.0 217.6 jit_solution(4050076900092081925)
XLA Ops:
  0.0 2.0 copy.57
  2.0 4.5 %all-to-all-start = ((bf16[128,8,256]{0,2,1:T(8,128)(2,1)}), bf16[128,8,256]{0,2,1:T(8,128)(2,1)S(1)}, u32[]{:S(2)}, u32[]{:S(2)}) async-start(bf16[128,8,256]{0,2,1:T(8,128)(2,1)} %bitcast.1), calls=%async_computation | async-start | bytes 1048576 | tf_op jit(solution)/shard_map/all_to_all | solution.py:54
  6.5 1.5 constant_dynamic-slice_fusion.3
  10.5 2.0 copy.63
  12.5 2.3 %copy.59 = bf16[128,4096]{0,1:T(8,128)(2,1)} copy(bf16[128,4096]{1,0:T(8,128)(2,1)} %param.5) | data formatting | bytes 2097152 | tf_op args[0]
  14.8 2.0 all-to-all-done
  16.8 3.5 %all-to-all-start.2 = ((bf16[128,8,256]{0,2,1:T(8,128)(2,1)}), bf16[128,8,256]{0,2,1:T(8,128)(2,1)S(1)}, u32[]{:S(2)}, u32[]{:S(2)}) async-start(bf16[128,8,256]{0,2,1:T(8,128)(2,1)} %bitcast.7), calls=%async_computation.2 | async-start | bytes 1048576 | tf_op jit(solution)/shard_map/all_to_all | solution.py:55
  22.0 8.6 %all-to-all-done.2 = bf16[128,8,256]{0,2,1:T(8,128)(2,1)S(1)} async-done(((bf16[128,8,256]{0,2,1:T(8,128)(2,1)}), bf16[128,8,256]{0,2,1:T(8,128)(2,1)S(1)}, u32[]{:S(2)}, u32[]{:S(2)}) %all-to-all-start.2) | async-done | bytes 524320 | tf_op jit(solution)/shard_map/all_to_all | solution.py:55
  30.6 4.2 %all-to-all-start.1 = ((bf16[128,8,512]{0,2,1:T(8,128)(2,1)}), bf16[128,8,512]{0,2,1:T(8,128)(2,1)}, u32[]{:S(2)}, u32[]{:S(2)}) async-start(bf16[128,8,512]{0,2,1:T(8,128)(2,1)} %bitcast.4), calls=%async_computation.1 | async-start | bytes 2097152 | tf_op jit(solution)/shard_map/all_to_all | solution.py:53
  35.7 4.9 %collective-permute-start.1 = (bf16[1024,512]{0,1:T(8,128)(2,1)}, bf16[1024,512]{0,1:T(8,128)(2,1)}, u32[]{:S(2)}, u32[]{:S(2)}) collective-permute-start(bf16[1024,512]{0,1:T(8,128)(2,1)} %bitcast_dynamic-update-slice_fusion), channel_id=1, source_target_pairs={{0,2},{1,3},{2,4},{3,5},{4,6},{5,7},{6,8},{7,9},{8,10},{9,11},{10,... | collective-permute-start | bytes 3145736 | tf_op jit(solution)/shard_map/ppermute | solution.py:16
  40.6 5.4 %and_and_fusion.3 = (pred[1024,1024]{0,1:T(8,128)(4,1)}, pred[1024,1024]{0,1:T(8,128)(4,1)S(1)}, pred[1024,1024]{0,1:T(8,128)(4,1)S(1)}, pred[1024,1024]{0,1:T(8,128)(4,1)}) fusion(s32[1024]{0:T(1024)S(1)} %iota_add_fusion.3, s32[1024]{0:T(1024)S(1)} %get-tuple-element.20, s32[1024]{0:T(1024)S(1)} %get-tuple-element.18, pred[]{:T(512)S(6)} %and.82, ...), kind=kLoop, calls=%fused_computation.31 | loop fusion | flops 16777216 | bytes 4231172 | tf_op jit(solution)/shard_map/and | solution.py:31
  46.0 3.5 %collective-permute-start.2 = (bf16[1024,512]{0,1:T(8,128)(2,1)}, bf16[1024,512]{0,1:T(8,128)(2,1)}, u32[]{:S(2)}, u32[]{:S(2)}) collective-permute-start(bf16[1024,512]{0,1:T(8,128)(2,1)} %bitcast_dynamic-update-slice_fusion), channel_id=1, source_target_pairs={{0,3},{1,4},{2,5},{3,6},{4,7},{5,8},{6,9},{7,10},{8,11},{9,12},{10... | collective-permute-start | bytes 3145736 | tf_op jit(solution)/shard_map/ppermute | solution.py:16
  49.5 2.8 %collective-permute-start = (bf16[1024,512]{0,1:T(8,128)(2,1)}, bf16[1024,512]{0,1:T(8,128)(2,1)}, u32[]{:S(2)}, u32[]{:S(2)}) collective-permute-start(bf16[1024,512]{0,1:T(8,128)(2,1)} %bitcast_dynamic-update-slice_fusion), channel_id=1, source_target_pairs={{0,1},{1,2},{2,3},{3,4},{4,5},{5,6},{6,7},{7,8},{8,9},{9,10},{10,1... | collective-permute-start | bytes 3145736 | tf_op jit(solution)/shard_map/ppermute | solution.py:16
  53.4 2.1 reshape.334
  56.9 1.9 copy.60
  58.8 1.3 reshape.335
  60.1 10.8 %fusion = (f32[1024,2,2]{0,2,1:T(2,128)S(1)}, f32[2,1024,1024,2]{2,1,3,0:T(8,128)}) fusion(pred[1024,1024]{0,1:T(8,128)(4,1)} %get-tuple-element.25, bf16[1024,2,2,128]{0,3,2,1:T(8,128)(2,1)} %reshape.335, bf16[1024,2,128]{0,2,1:T(8,128)(2,1)} %reshape.334), kind=kOutput, calls=%fused_computation.8 | convolution fusion | flops 1086320640 | bytes 19415040 | tf_op jit(solution)/shard_map/qgmd,kgd->qgmk/dot_general | solution.py:27
  70.8 2.1 fusion.51
  72.9 7.5 %fusion.2 = (f32[1024,2,2]{0,2,1:T(2,128)S(1)}, f32[2,1024,1024,2]{2,1,3,0:T(8,128)}) fusion(pred[1024,1024]{0,1:T(8,128)(4,1)S(1)} %get-tuple-element.26, bf16[1024,2,128,1]{0,2,3,1:T(8,128)(2,1)S(1)} %bitcast.168, bf16[1024,2,2,128]{0,3,2,1:T(8,128)(2,1)S(1)} %copy-done.1), kind=kOutput, calls=%fused_computation.10 | convolution fusion | flops 1086320640 | bytes 19415040 | tf_op jit(solution)/shard_map/qgmd,kgd->qgmk/dot_general | solution.py:27
  80.5 2.1 fusion.49
  82.6 7.5 %fusion.3 = (f32[1024,2,2]{0,2,1:T(2,128)S(1)}, f32[2,1024,1024,2]{2,1,3,0:T(8,128)}) fusion(pred[1024,1024]{0,1:T(8,128)(4,1)S(1)} %get-tuple-element.27, bf16[1024,2,128,1]{0,2,3,1:T(8,128)(2,1)S(1)} %bitcast.169, bf16[1024,2,2,128]{0,3,2,1:T(8,128)(2,1)S(1)} %copy-done.1), kind=kOutput, calls=%fused_computation.11 | convolution fusion | flops 1086320640 | bytes 19415040 | tf_op jit(solution)/shard_map/qgmd,kgd->qgmk/dot_general | solution.py:27
  90.2 22.5 %collective-permute-done = bf16[1024,512]{0,1:T(8,128)(2,1)} collective-permute-done((bf16[1024,512]{0,1:T(8,128)(2,1)}, bf16[1024,512]{0,1:T(8,128)(2,1)}, u32[]{:S(2)}, u32[]{:S(2)}) %collective-permute-start) | collective-permute-done | bytes 1048608 | tf_op jit(solution)/shard_map/ppermute | solution.py:16
  112.7 2.1 fusion.50
  114.7 7.6 %fusion.1 = (f32[1024,2,2]{0,2,1:T(2,128)S(1)}, f32[2,1024,1024,2]{2,1,3,0:T(8,128)}) fusion(pred[1024,1024]{0,1:T(8,128)(4,1)S(1)} %copy-done, bf16[1024,2,128,1]{0,2,3,1:T(8,128)(2,1)S(1)} %bitcast.167, bf16[1024,2,2,128]{0,3,2,1:T(8,128)(2,1)S(1)} %copy-done.1), kind=kOutput, calls=%fused_computation.9 | convolution fusion | flops 1086320640 | bytes 19415040 | tf_op jit(solution)/shard_map/qgmd,kgd->qgmk/dot_general | solution.py:27
  122.3 13.5 %fusion.18 = f32[2,1024,2,128]{3,1,2,0:T(8,128)} fusion(f32[2,1024,1024,2]{2,1,3,0:T(8,128)} %get-tuple-element.40, f32[1024,2,2]{0,2,1:T(2,128)S(1)} %get-tuple-element.24, pred[1024,1024]{0,1:T(8,128)(4,1)} %get-tuple-element.25, bf16[1024,2,128]{0,2,1:T(8,128)(2,1)} %reshape.336), kind=kOutput, calls=%fused_computation.23 | convolution fusion | flops 1094713344 | bytes 20463616 | tf_op jit(solution)/shard_map/qgmk,kgd->qgmd/dot_general | solution.py:41
  135.9 14.0 %fusion.4 = (f32[1024,2,2]{0,2,1:T(2,128)S(1)}, f32[1024,2,2]{0,2,1:T(2,128)S(1)}) fusion(f32[2,1024,1024,2]{2,1,3,0:T(8,128)} %get-tuple-element.40, f32[1024,2,2]{0,2,1:T(2,128)S(1)} %get-tuple-element.24, pred[1024,1024]{0,1:T(8,128)(4,1)} %get-tuple-element.25, f32[1024,2,2]{0,2,1:T(2,128)S(1)} %get-tuple-element.11, ...), kind=kLoop, calls=%fused_computation.12 | loop fusion | flops 41934848 | bytes 35717120 | tf_op jit(solution)/shard_map/reduce_sum | solution.py:40
  149.9 10.7 %fusion.16 = f32[2,128,1024,2]{1,2,3,0:T(8,128)} fusion(bf16[1024,2,128,1]{0,2,3,1:T(8,128)(2,1)S(1)} %bitcast.166, f32[2,1024,1024,2]{2,1,3,0:T(8,128)} %get-tuple-element.38, f32[1024,2,2]{0,2,1:T(2,128)S(1)} %get-tuple-element.11, pred[1024,1024]{0,1:T(8,128)(4,1)S(1)} %copy-done), kind=kOutput, calls=%fused_computation.22 | convolution fusion | flops 1094713344 | bytes 20463616 | tf_op jit(solution)/shard_map/qgmk,kgd->qgmd/dot_general | solution.py:41
  160.6 11.0 %fusion.14 = f32[2,128,1024,2]{1,2,3,0:T(8,128)} fusion(bf16[1024,2,128,1]{0,2,3,1:T(8,128)(2,1)S(1)} %bitcast.165, f32[2,1024,1024,2]{2,1,3,0:T(8,128)} %get-tuple-element.36, f32[1024,2,2]{0,2,1:T(2,128)S(1)} %get-tuple-element.10, pred[1024,1024]{0,1:T(8,128)(4,1)S(1)} %get-tuple-element.26), kind=kOutput, calls=%fused_computation.21 | convolution fusion | flops 1094713344 | bytes 20463616 | tf_op jit(solution)/shard_map/qgmk,kgd->qgmd/dot_general | solution.py:41
  171.6 14.7 %fusion.8 = (f32[1024,2,2]{0,2,1:T(2,128)S(1)}, f32[1024,2,2]{0,2,1:T(2,128)S(1)}) fusion(f32[2,1024,1024,2]{2,1,3,0:T(8,128)} %get-tuple-element.36, f32[1024,2,2]{0,2,1:T(2,128)S(1)} %get-tuple-element.10, pred[1024,1024]{0,1:T(8,128)(4,1)S(1)} %get-tuple-element.26, f32[1024,2,2]{0,2,1:T(2,128)S(1)} %get-tuple-element.9, ...), kind=kLoop, calls=%fused_computation.16 | loop fusion | flops 41934848 | bytes 35717120 | tf_op jit(solution)/shard_map/reduce_sum | solution.py:40
  186.8 8.3 %fusion.25 = bf16[1024,2,2,128]{3,0,2,1:T(8,128)(2,1)S(1)} fusion(f32[2,128,1024,2]{1,2,3,0:T(8,128)S(1)} %copy-done.7, f32[2,128,1024,2]{1,2,3,0:T(8,128)S(1)} %copy-done.6, f32[2,1024,2,128]{3,1,2,0:T(8,128)S(1)} %copy-done.5, bf16[1024,2,128,1]{0,2,3,1:T(8,128)(2,1)S(1)} %bitcast.164, f32[2,1024,1024,2]{2,1,3,0:T(8,128)S(1)} %bitcast.158, ...), kind=kOutput, calls=%fused_computation.34 | convolution fusion | flops 1099431936 | bytes 25788416 | tf_op jit(solution)/shard_map/qgmk,kgd->qgmd/dot_general | solution.py:41
  196.1 20.2 %all_to_all.73 = bf16[8,128,512]{1,2,0:T(8,128)(2,1)S(1)} all-to-all(bf16[8,128,512]{1,2,0:T(8,128)(2,1)S(1)} %copy.82), channel_id=1, replica_groups=mesh['head'=8,'ctx'=32] {'head'}, dimensions={0} | all-to-all | bytes 2097152 | tf_op jit(solution)/shard_map/all_to_all | solution.py:98
  216.3 1.3 copy.83
  (43 shorter events, 6.5 us)
Async XLA Ops:
  2.0 14.8 %all-to-all-start = ((bf16[128,8,256]{0,2,1:T(8,128)(2,1)}), bf16[128,8,256]{0,2,1:T(8,128)(2,1)S(1)}, u32[]{:S(2)}, u32[]{:S(2)}) async-start(bf16[128,8,256]{0,2,1:T(8,128)(2,1)} %bitcast.1), calls=%async_computation | async-start | bytes 1048576 | tf_op jit(solution)/shard_map/all_to_all | solution.py:54
  16.8 13.7 %all-to-all-start.2 = ((bf16[128,8,256]{0,2,1:T(8,128)(2,1)}), bf16[128,8,256]{0,2,1:T(8,128)(2,1)S(1)}, u32[]{:S(2)}, u32[]{:S(2)}) async-start(bf16[128,8,256]{0,2,1:T(8,128)(2,1)} %bitcast.7), calls=%async_computation.2 | async-start | bytes 1048576 | tf_op jit(solution)/shard_map/all_to_all | solution.py:55
  30.6 26.3 %all-to-all-start.1 = ((bf16[128,8,512]{0,2,1:T(8,128)(2,1)}), bf16[128,8,512]{0,2,1:T(8,128)(2,1)}, u32[]{:S(2)}, u32[]{:S(2)}) async-start(bf16[128,8,512]{0,2,1:T(8,128)(2,1)} %bitcast.4), calls=%async_computation.1 | async-start | bytes 2097152 | tf_op jit(solution)/shard_map/all_to_all | solution.py:53
  35.7 35.1 %collective-permute-start.1 = (bf16[1024,512]{0,1:T(8,128)(2,1)}, bf16[1024,512]{0,1:T(8,128)(2,1)}, u32[]{:S(2)}, u32[]{:S(2)}) collective-permute-start(bf16[1024,512]{0,1:T(8,128)(2,1)} %bitcast_dynamic-update-slice_fusion), channel_id=1, source_target_pairs={{0,2},{1,3},{2,4},{3,5},{4,6},{5,7},{6,8},{7,9},{8,10},{9,11},{10,... | collective-permute-start | bytes 3145736 | tf_op jit(solution)/shard_map/ppermute | solution.py:16
  46.0 34.5 %collective-permute-start.2 = (bf16[1024,512]{0,1:T(8,128)(2,1)}, bf16[1024,512]{0,1:T(8,128)(2,1)}, u32[]{:S(2)}, u32[]{:S(2)}) collective-permute-start(bf16[1024,512]{0,1:T(8,128)(2,1)} %bitcast_dynamic-update-slice_fusion), channel_id=1, source_target_pairs={{0,3},{1,4},{2,5},{3,6},{4,7},{5,8},{6,9},{7,10},{8,11},{9,12},{10... | collective-permute-start | bytes 3145736 | tf_op jit(solution)/shard_map/ppermute | solution.py:16
  49.5 63.2 %collective-permute-start = (bf16[1024,512]{0,1:T(8,128)(2,1)}, bf16[1024,512]{0,1:T(8,128)(2,1)}, u32[]{:S(2)}, u32[]{:S(2)}) collective-permute-start(bf16[1024,512]{0,1:T(8,128)(2,1)} %bitcast_dynamic-update-slice_fusion), channel_id=1, source_target_pairs={{0,1},{1,2},{2,3},{3,4},{4,5},{5,6},{6,7},{7,8},{8,9},{9,10},{10,1... | collective-permute-start | bytes 3145736 | tf_op jit(solution)/shard_map/ppermute | solution.py:16
  60.1 12.9 %copy-start.1 = (bf16[1024,2,2,128]{0,3,2,1:T(8,128)(2,1)S(1)}, bf16[1024,2,2,128]{0,3,2,1:T(8,128)(2,1)}, u32[]{:S(2)}) copy-start(bf16[1024,2,2,128]{0,3,2,1:T(8,128)(2,1)} %reshape.335) | copy-start | bytes 3145732
  80.5 34.3 %copy-start = (pred[1024,1024]{0,1:T(8,128)(4,1)S(1)}, pred[1024,1024]{0,1:T(8,128)(4,1)}, u32[]{:S(2)}) copy-start(pred[1024,1024]{0,1:T(8,128)(4,1)} %get-tuple-element.28) | copy-start | bytes 3145732
  135.9 14.0 %copy-start.4 = (bf16[1024,256]{0,1:T(8,128)(2,1)S(1)}, bf16[1024,256]{0,1:T(8,128)(2,1)}, u32[]{:S(2)}) copy-start(bf16[1024,256]{0,1:T(8,128)(2,1)} %get-tuple-element.14) | copy-start | bytes 1572868
  149.9 10.7 %copy-start.3 = (bf16[1024,256]{0,1:T(8,128)(2,1)S(1)}, bf16[1024,256]{0,1:T(8,128)(2,1)}, u32[]{:S(2)}) copy-start(bf16[1024,256]{0,1:T(8,128)(2,1)} %get-tuple-element.17) | copy-start | bytes 1572868
  160.6 25.8 %slice-start = ((s8[16777216]{0:T(1024)(128)(4,1)}), s8[4194304]{0:T(1024)(128)(4,1)S(1)}, s32[]{:S(2)}) async-start(s8[16777216]{0:T(1024)(128)(4,1)} %bitcast.157), calls=%async_computation.4 | async-start | bytes 8388608
  160.6 25.8 %slice-start.1 = ((s8[16777216]{0:T(1024)(128)(4,1)}), s8[4194304]{0:T(1024)(128)(4,1)S(1)}, s32[]{:S(2)}) async-start(s8[16777216]{0:T(1024)(128)(4,1)} %bitcast.157), calls=%async_computation.5 | async-start | bytes 8388608
  171.6 14.8 %slice-start.2 = ((s8[16777216]{0:T(1024)(128)(4,1)}), s8[4194304]{0:T(1024)(128)(4,1)S(1)}, s32[]{:S(2)}) async-start(s8[16777216]{0:T(1024)(128)(4,1)} %bitcast.157), calls=%async_computation.6 | async-start | bytes 8388608
  171.6 14.8 %slice-start.3 = ((s8[16777216]{0:T(1024)(128)(4,1)}), s8[4194304]{0:T(1024)(128)(4,1)S(1)}, s32[]{:S(2)}) async-start(s8[16777216]{0:T(1024)(128)(4,1)} %bitcast.157), calls=%async_computation.7 | async-start | bytes 8388608
  171.6 14.8 %copy-start.2 = (bf16[1024,256]{0,1:T(8,128)(2,1)S(1)}, bf16[1024,256]{0,1:T(8,128)(2,1)}, u32[]{:S(2)}) copy-start(bf16[1024,256]{0,1:T(8,128)(2,1)} %get-tuple-element.12) | copy-start | bytes 1572868
  171.6 14.8 %copy-start.5 = (f32[2,1024,2,128]{3,1,2,0:T(8,128)S(1)}, f32[2,1024,2,128]{3,1,2,0:T(8,128)}, u32[]{:S(2)}) copy-start(f32[2,1024,2,128]{3,1,2,0:T(8,128)} %fusion.18) | copy-start | bytes 6291460
  171.6 14.8 %copy-start.6 = (f32[2,128,1024,2]{1,2,3,0:T(8,128)S(1)}, f32[2,128,1024,2]{1,2,3,0:T(8,128)}, u32[]{:S(2)}) copy-start(f32[2,128,1024,2]{1,2,3,0:T(8,128)} %fusion.16) | copy-start | bytes 6291460
  171.6 15.1 %copy-start.7 = (f32[2,128,1024,2]{1,2,3,0:T(8,128)S(1)}, f32[2,128,1024,2]{1,2,3,0:T(8,128)}, u32[]{:S(2)}) copy-start(f32[2,128,1024,2]{1,2,3,0:T(8,128)} %fusion.14) | copy-start | bytes 6291460
where the time goes:
time: 218 us
  matrix products  77 us (35%)
  other arithmetic  34.2 us (16%)
  waiting for transfers between devices  33.1 us (15%)
  local copies, waits for them, and re-layouts  27 us (12%)
  starting transfers between devices  23.4 us (11%)
  blocking collectives  20.2 us (9%)
  between operations  2.73 us (1%)
    dot_general x4, matrix products, attend_block(): jnp.einsum('qgmk,kgd->qgmd', weights.astype(jnp.bfloat16), value_part, pr...  43.6 us
    dot_general x4, matrix products, attend_block(): jnp.einsum('qgmd,kgd->qgmk', grouped, key_part, preferred_element_type=jn...  33.4 us
    reduce_sum x2, other arithmetic, attend_block(): totals = totals * rescale + jnp.sum(weights, axis=3)  28.7 us
    ppermute x3, waiting for transfers between devices, passed_along(): lax.ppermute(value, axis, [(source, source + steps) for source in range(l...  22.5 us
    all_to_all x1, blocking collectives, per_device(): lax.all_to_all(outputs, 'head', split_axis=0, concat_axis=1, tiled=True)  20.2 us
    ppermute x3, starting transfers between devices, passed_along(): lax.ppermute(value, axis, [(source, source + steps) for source in range(l...  11.2 us
    all_to_all x1, waiting for transfers between devices, per_device(): lax.all_to_all(value_matrix, 'head', split_axis=1, concat_axis=0, tiled=T...  8.57 us
    unnamed x29, local copies, waits for them, and re-layouts  7.82 us
  transfers between devices with their start and end apart: 6, of which 3 were waited for; matrix products, arithmetic and copies ran while one was open for 24% of the time, Pallas kernels for 0%

commit v1 on v0

--- a/solution.py
+++ b/solution.py
@@ -95,7 +95,10 @@
         .astype(jnp.bfloat16)
         .reshape(rows_per_block, heads_local * query_group_width * HEAD_WIDTH)
     )
-    return lax.all_to_all(outputs, "head", split_axis=0, concat_axis=1, tiled=True)
+    return jnp.concatenate(
+        lax.all_to_all(jnp.stack(jnp.split(outputs, lax.axis_size("head"), axis=0)), "head", 0, 0),
+        axis=1,
+    )
 
 
 def solution(mesh):

time: 218 us -> 207 us (0.950)
  matrix products: 77 us -> 66.6 us
  other arithmetic: 34.2 us -> 30.2 us
  waiting for transfers between devices: 33.1 us -> 36.6 us
    dot_general x4, matrix products: 43.6 us -> 37.4 us  [attend_block(): jnp.einsum('qgmk,kgd->qgmd', weights.astype(jnp.bfloat16), value_part, pr...]
    dot_general x4, matrix products: 33.4 us -> 29.3 us  [attend_block(): jnp.einsum('qgmd,kgd->qgmk', grouped, key_part, preferred_element_type=jn...]
    reduce_sum x2, other arithmetic: 28.7 us -> 24.6 us  [attend_block(): totals = totals * rescale + jnp.sum(weights, axis=3)]
    ppermute x3, waiting for transfers between devices: 22.5 us -> 26.1 us  [passed_along(): lax.ppermute(value, axis, [(source, source + steps) for source in range(l...]
    unnamed x29 -> x21, local copies, waits for them, and re-layouts: 7.82 us -> 7.37 us
  transfers between devices with their start and end apart: 6 -> 6, of which waited for: 3 -> 3; matrix products, arithmetic and copies ran while one was open for 24% -> 23% of each run, Pallas kernels for 0% -> 0%
where the time goes in v1:
time: 207 us; the launch traced here: 206 us
  matrix products  66.6 us (32%)
  waiting for transfers between devices  36.6 us (18%)
  other arithmetic  30.2 us (15%)
  local copies, waits for them, and re-layouts  26.6 us (13%)
  starting transfers between devices  23.4 us (11%)
  blocking collectives  20.2 us (10%)
  between operations  2.74 us (1%)
    dot_general x4, matrix products, attend_block(): jnp.einsum('qgmk,kgd->qgmd', weights.astype(jnp.bfloat16), value_part, pr...  37.4 us
    dot_general x4, matrix products, attend_block(): jnp.einsum('qgmd,kgd->qgmk', grouped, key_part, preferred_element_type=jn...  29.3 us
    ppermute x3, waiting for transfers between devices, passed_along(): lax.ppermute(value, axis, [(source, source + steps) for source in range(l...  26.1 us
    reduce_sum x2, other arithmetic, attend_block(): totals = totals * rescale + jnp.sum(weights, axis=3)  24.6 us
    all_to_all x1, blocking collectives, per_device(): lax.all_to_all(jnp.stack(jnp.split(outputs, lax.axis_size('head'), axis=0...  20.2 us
    ppermute x3, starting transfers between devices, passed_along(): lax.ppermute(value, axis, [(source, source + steps) for source in range(l...  11.2 us
    all_to_all x1, waiting for transfers between devices, per_device(): lax.all_to_all(value_matrix, 'head', split_axis=1, concat_axis=0, tiled=T...  8.57 us
    unnamed x21, local copies, waits for them, and re-layouts  7.37 us
  transfers between devices with their start and end apart: 6, of which 3 were waited for; matrix products, arithmetic and copies ran while one was open for 23% of the time, Pallas kernels for 0%

profile of v1, /device:TPU:128, one launch (start us, length us, event | category | flops | bytes accessed | tf_op | source)
XLA Modules:
  0.0 206.4 jit_solution(7923619695191297150)
XLA Ops:
  0.0 2.0 copy.29
  2.0 4.5 %all-to-all-start = ((bf16[128,8,256]{0,2,1:T(8,128)(2,1)}), bf16[128,8,256]{0,2,1:T(8,128)(2,1)S(1)}, u32[]{:S(2)}, u32[]{:S(2)}) async-start(bf16[128,8,256]{0,2,1:T(8,128)(2,1)} %bitcast.1), calls=%async_computation | async-start | bytes 1048576 | tf_op jit(solution)/shard_map/all_to_all | solution.py:54
  6.5 1.5 constant_dynamic-slice_fusion.3
  10.5 2.0 copy.35
  12.5 2.3 %copy.31 = bf16[128,4096]{0,1:T(8,128)(2,1)} copy(bf16[128,4096]{1,0:T(8,128)(2,1)} %param.5) | data formatting | bytes 2097152 | tf_op args[0]
  14.8 2.0 all-to-all-done
  16.8 3.5 %all-to-all-start.2 = ((bf16[128,8,256]{0,2,1:T(8,128)(2,1)}), bf16[128,8,256]{0,2,1:T(8,128)(2,1)S(1)}, u32[]{:S(2)}, u32[]{:S(2)}) async-start(bf16[128,8,256]{0,2,1:T(8,128)(2,1)} %bitcast.7), calls=%async_computation.2 | async-start | bytes 1048576 | tf_op jit(solution)/shard_map/all_to_all | solution.py:55
  22.0 8.6 %all-to-all-done.2 = bf16[128,8,256]{0,2,1:T(8,128)(2,1)S(1)} async-done(((bf16[128,8,256]{0,2,1:T(8,128)(2,1)}), bf16[128,8,256]{0,2,1:T(8,128)(2,1)S(1)}, u32[]{:S(2)}, u32[]{:S(2)}) %all-to-all-start.2) | async-done | bytes 524320 | tf_op jit(solution)/shard_map/all_to_all | solution.py:55
  30.6 4.2 %all-to-all-start.1 = ((bf16[128,8,512]{0,2,1:T(8,128)(2,1)}), bf16[128,8,512]{0,2,1:T(8,128)(2,1)}, u32[]{:S(2)}, u32[]{:S(2)}) async-start(bf16[128,8,512]{0,2,1:T(8,128)(2,1)} %bitcast.4), calls=%async_computation.1 | async-start | bytes 2097152 | tf_op jit(solution)/shard_map/all_to_all | solution.py:53
  35.7 4.9 %collective-permute-start.1 = (bf16[1024,512]{0,1:T(8,128)(2,1)}, bf16[1024,512]{0,1:T(8,128)(2,1)}, u32[]{:S(2)}, u32[]{:S(2)}) collective-permute-start(bf16[1024,512]{0,1:T(8,128)(2,1)} %bitcast_dynamic-update-slice_fusion), channel_id=1, source_target_pairs={{0,2},{1,3},{2,4},{3,5},{4,6},{5,7},{6,8},{7,9},{8,10},{9,11},{10,... | collective-permute-start | bytes 3145736 | tf_op jit(solution)/shard_map/ppermute | solution.py:16
  40.6 5.4 %and_and_fusion.3 = (pred[1024,1024]{0,1:T(8,128)(4,1)}, pred[1024,1024]{0,1:T(8,128)(4,1)S(1)}, pred[1024,1024]{0,1:T(8,128)(4,1)S(1)}, pred[1024,1024]{0,1:T(8,128)(4,1)}) fusion(s32[1024]{0:T(1024)S(1)} %iota_add_fusion.3, s32[1024]{0:T(1024)S(1)} %get-tuple-element.28, s32[1024]{0:T(1024)S(1)} %get-tuple-element.26, pred[]{:T(512)S(6)} %and.82, ...), kind=kLoop, calls=%fused_computation.31 | loop fusion | flops 16777216 | bytes 4231172 | tf_op jit(solution)/shard_map/and | solution.py:31
  46.1 3.5 %collective-permute-start.2 = (bf16[1024,512]{0,1:T(8,128)(2,1)}, bf16[1024,512]{0,1:T(8,128)(2,1)}, u32[]{:S(2)}, u32[]{:S(2)}) collective-permute-start(bf16[1024,512]{0,1:T(8,128)(2,1)} %bitcast_dynamic-update-slice_fusion), channel_id=1, source_target_pairs={{0,3},{1,4},{2,5},{3,6},{4,7},{5,8},{6,9},{7,10},{8,11},{9,12},{10... | collective-permute-start | bytes 3145736 | tf_op jit(solution)/shard_map/ppermute | solution.py:16
  49.6 2.8 %collective-permute-start = (bf16[1024,512]{0,1:T(8,128)(2,1)}, bf16[1024,512]{0,1:T(8,128)(2,1)}, u32[]{:S(2)}, u32[]{:S(2)}) collective-permute-start(bf16[1024,512]{0,1:T(8,128)(2,1)} %bitcast_dynamic-update-slice_fusion), channel_id=1, source_target_pairs={{0,1},{1,2},{2,3},{3,4},{4,5},{5,6},{6,7},{7,8},{8,9},{9,10},{10,1... | collective-permute-start | bytes 3145736 | tf_op jit(solution)/shard_map/ppermute | solution.py:16
  53.5 2.1 %reshape.352 = bf16[1024,2,128]{0,2,1:T(8,128)(2,1)} reshape(bf16[8,128,256]{1,0,2:T(8,128)(2,1)} %copy.30) | data formatting | bytes 1048576 | tf_op jit(solution)/shard_map/reshape | solution.py:22
  56.2 2.9 %copy.32 = bf16[8,128,512]{1,0,2:T(8,128)(2,1)} copy(bf16[8,128,512]{1,2,0:T(8,128)(2,1)} %bitcast.5) | data formatting | bytes 2097152 | tf_op jit(solution)/shard_map/all_to_all | solution.py:53
  59.1 2.3 %reshape.353 = bf16[1024,2,2,128]{0,3,2,1:T(8,128)(2,1)} reshape(bf16[8,128,512]{1,0,2:T(8,128)(2,1)} %copy.32) | data formatting | bytes 2097152 | tf_op jit(solution)/shard_map/reshape | solution.py:70
  61.4 10.8 %fusion = (f32[1024,2,2]{0,2,1:T(2,128)S(1)}, f32[2,1024,1024,2]{2,1,3,0:T(8,128)}) fusion(pred[1024,1024]{0,1:T(8,128)(4,1)} %get-tuple-element.33, bf16[1024,2,2,128]{0,3,2,1:T(8,128)(2,1)} %reshape.353, bf16[1024,2,128]{0,2,1:T(8,128)(2,1)} %reshape.352), kind=kOutput, calls=%fused_computation.8 | convolution fusion | flops 1086320640 | bytes 19415040 | tf_op jit(solution)/shard_map/qgmd,kgd->qgmk/dot_general | solution.py:27
  72.2 2.1 %fusion.52 = (bf16[1024,256]{0,1:T(8,128)(2,1)S(1)}, bf16[1024,256]{0,1:T(8,128)(2,1)}) fusion(bf16[1024,512]{0,1:T(8,128)(2,1)} %collective-permute-done.1), kind=kLoop, calls=%fused_computation.85 | loop fusion | bytes 2097152 | tf_op jit(solution)/shard_map/slice | solution.py:22
  74.3 7.6 %fusion.2 = (f32[1024,2,2]{0,2,1:T(2,128)S(1)}, f32[2,1024,1024,2]{2,1,3,0:T(8,128)}) fusion(pred[1024,1024]{0,1:T(8,128)(4,1)S(1)} %get-tuple-element.34, bf16[1024,2,128,1]{0,2,3,1:T(8,128)(2,1)S(1)} %bitcast.172, bf16[1024,2,2,128]{0,3,2,1:T(8,128)(2,1)S(1)} %copy-done.2), kind=kOutput, calls=%fused_computation.10 | convolution fusion | flops 1086320640 | bytes 19415040 | tf_op jit(solution)/shard_map/qgmd,kgd->qgmk/dot_general | solution.py:27
  81.8 1.4 fusion.50
  83.2 3.4 %fusion.3 = (f32[1024,2,2]{0,2,1:T(2,128)S(1)}, f32[2,1024,1024,2]{2,1,3,0:T(8,128)S(1)}) fusion(pred[1024,1024]{0,1:T(8,128)(4,1)S(1)} %get-tuple-element.35, bf16[1024,2,128,1]{0,2,3,1:T(8,128)(2,1)S(1)} %bitcast.173, bf16[1024,2,2,128]{0,3,2,1:T(8,128)(2,1)S(1)} %copy-done.2), kind=kOutput, calls=%fused_computation.11 | convolution fusion | flops 1086320640 | bytes 19415040 | tf_op jit(solution)/shard_map/qgmd,kgd->qgmk/dot_general | solution.py:27
  86.6 26.1 %collective-permute-done = bf16[1024,512]{0,1:T(8,128)(2,1)} collective-permute-done((bf16[1024,512]{0,1:T(8,128)(2,1)}, bf16[1024,512]{0,1:T(8,128)(2,1)}, u32[]{:S(2)}, u32[]{:S(2)}) %collective-permute-start) | collective-permute-done | bytes 1048608 | tf_op jit(solution)/shard_map/ppermute | solution.py:16
  112.7 2.1 fusion.51
  114.7 7.5 %fusion.1 = (f32[1024,2,2]{0,2,1:T(2,128)S(1)}, f32[2,1024,1024,2]{2,1,3,0:T(8,128)}) fusion(pred[1024,1024]{0,1:T(8,128)(4,1)S(1)} %copy-done, bf16[1024,2,128,1]{0,2,3,1:T(8,128)(2,1)S(1)} %bitcast.171, bf16[1024,2,2,128]{0,3,2,1:T(8,128)(2,1)S(1)} %copy-done.2), kind=kOutput, calls=%fused_computation.9 | convolution fusion | flops 1086320640 | bytes 19415040 | tf_op jit(solution)/shard_map/qgmd,kgd->qgmk/dot_general | solution.py:27
  122.3 10.2 %fusion.18 = f32[2,1024,2,128]{1,3,2,0:T(8,128)} fusion(f32[2,1024,1024,2]{2,1,3,0:T(8,128)} %get-tuple-element.48, f32[1024,2,2]{0,2,1:T(2,128)S(1)} %get-tuple-element.32, pred[1024,1024]{0,1:T(8,128)(4,1)S(1)} %copy-done.1, bf16[1024,2,128,1]{0,2,1,3:T(8,128)(2,1)S(1)} %reshape.364), kind=kOutput, calls=%fused_computation.23 | convolution fusion | flops 1094713344 | bytes 20463616 | tf_op jit(solution)/shard_map/qgmk,kgd->qgmd/dot_general | solution.py:41
  132.6 13.7 %fusion.4 = (f32[1024,2,2]{0,2,1:T(2,128)S(1)}, f32[1024,2,2]{0,2,1:T(2,128)S(1)}) fusion(f32[2,1024,1024,2]{2,1,3,0:T(8,128)} %get-tuple-element.48, f32[1024,2,2]{0,2,1:T(2,128)S(1)} %get-tuple-element.32, pred[1024,1024]{0,1:T(8,128)(4,1)S(1)} %copy-done.1, f32[1024,2,2]{0,2,1:T(2,128)S(1)} %get-tuple-element.11, ...), kind=kLoop, calls=%fused_computation.12 | loop fusion | flops 41934848 | bytes 35717120 | tf_op jit(solution)/shard_map/reduce_sum | solution.py:40
  146.3 10.1 %fusion.16 = f32[2,128,1024,2]{2,1,3,0:T(8,128)} fusion(bf16[1024,2,128,1]{0,2,3,1:T(8,128)(2,1)S(1)} %bitcast.170, f32[2,1024,1024,2]{2,1,3,0:T(8,128)} %get-tuple-element.46, f32[1024,2,2]{0,2,1:T(2,128)S(1)} %get-tuple-element.11, pred[1024,1024]{0,1:T(8,128)(4,1)S(1)} %copy-done), kind=kOutput, calls=%fused_computation.22 | convolution fusion | flops 1094713344 | bytes 20463616 | tf_op jit(solution)/shard_map/qgmk,kgd->qgmd/dot_general | solution.py:41
  156.4 9.9 %fusion.14 = f32[2,128,1024,2]{2,1,3,0:T(8,128)} fusion(bf16[1024,2,128,1]{0,2,3,1:T(8,128)(2,1)S(1)} %bitcast.169, f32[2,1024,1024,2]{2,1,3,0:T(8,128)} %get-tuple-element.44, f32[1024,2,2]{0,2,1:T(2,128)S(1)} %get-tuple-element.10, pred[1024,1024]{0,1:T(8,128)(4,1)S(1)} %get-tuple-element.34), kind=kOutput, calls=%fused_computation.21 | convolution fusion | flops 1094713344 | bytes 20463616 | tf_op jit(solution)/shard_map/qgmk,kgd->qgmd/dot_general | solution.py:41
  166.3 10.9 %fusion.8 = (f32[1024,2,2]{0,2,1:T(2,128)S(1)}, f32[1024,2,2]{0,2,1:T(2,128)S(1)}) fusion(f32[2,1024,1024,2]{2,1,3,0:T(8,128)} %get-tuple-element.44, f32[1024,2,2]{0,2,1:T(2,128)S(1)} %get-tuple-element.10, pred[1024,1024]{0,1:T(8,128)(4,1)S(1)} %get-tuple-element.34, f32[1024,2,2]{0,2,1:T(2,128)S(1)} %get-tuple-element.9, ...), kind=kLoop, calls=%fused_computation.16 | loop fusion | flops 41934848 | bytes 35717120 | tf_op jit(solution)/shard_map/reduce_sum | solution.py:40
  177.3 7.2 %fusion.25 = bf16[1024,2,2,128]{0,3,2,1:T(8,128)(2,1)S(1)} fusion(f32[2,128,1024,2]{2,1,3,0:T(8,128)} %fusion.14, f32[2,128,1024,2]{2,1,3,0:T(8,128)} %fusion.16, f32[2,1024,2,128]{1,3,2,0:T(8,128)} %fusion.18, bf16[1024,2,128,1]{0,2,3,1:T(8,128)(2,1)S(1)} %bitcast.168, f32[2,1024,1024,2]{2,1,3,0:T(8,128)S(1)} %get-tuple-element.42, ...), kind=kOutput, calls=%fused_computation.34 | convolution fusion | flops 1099431936 | bytes 25788416 | tf_op jit(solution)/shard_map/qgmk,kgd->qgmd/dot_general | solution.py:41
  184.9 20.2 %all_to_all.59 = bf16[8,128,512]{1,2,0:T(8,128)(2,1)S(1)} all-to-all(bf16[8,128,512]{1,2,0:T(8,128)(2,1)S(1)} %constant_dynamic-update-slice_fusion), channel_id=1, replica_groups=mesh['head'=8,'ctx'=32] {'head'}, dimensions={0} | all-to-all | bytes 2097152 | tf_op jit(solution)/shard_map/all_to_all | solution.py:99
  205.1 1.3 copy.74
  (34 shorter events, 4.8 us)
Async XLA Ops:
  2.0 14.8 %all-to-all-start = ((bf16[128,8,256]{0,2,1:T(8,128)(2,1)}), bf16[128,8,256]{0,2,1:T(8,128)(2,1)S(1)}, u32[]{:S(2)}, u32[]{:S(2)}) async-start(bf16[128,8,256]{0,2,1:T(8,128)(2,1)} %bitcast.1), calls=%async_computation | async-start | bytes 1048576 | tf_op jit(solution)/shard_map/all_to_all | solution.py:54
  16.8 13.7 %all-to-all-start.2 = ((bf16[128,8,256]{0,2,1:T(8,128)(2,1)}), bf16[128,8,256]{0,2,1:T(8,128)(2,1)S(1)}, u32[]{:S(2)}, u32[]{:S(2)}) async-start(bf16[128,8,256]{0,2,1:T(8,128)(2,1)} %bitcast.7), calls=%async_computation.2 | async-start | bytes 1048576 | tf_op jit(solution)/shard_map/all_to_all | solution.py:55
  30.6 25.6 %all-to-all-start.1 = ((bf16[128,8,512]{0,2,1:T(8,128)(2,1)}), bf16[128,8,512]{0,2,1:T(8,128)(2,1)}, u32[]{:S(2)}, u32[]{:S(2)}) async-start(bf16[128,8,512]{0,2,1:T(8,128)(2,1)} %bitcast.4), calls=%async_computation.1 | async-start | bytes 2097152 | tf_op jit(solution)/shard_map/all_to_all | solution.py:53
  35.7 36.5 %collective-permute-start.1 = (bf16[1024,512]{0,1:T(8,128)(2,1)}, bf16[1024,512]{0,1:T(8,128)(2,1)}, u32[]{:S(2)}, u32[]{:S(2)}) collective-permute-start(bf16[1024,512]{0,1:T(8,128)(2,1)} %bitcast_dynamic-update-slice_fusion), channel_id=1, source_target_pairs={{0,2},{1,3},{2,4},{3,5},{4,6},{5,7},{6,8},{7,9},{8,10},{9,11},{10,... | collective-permute-start | bytes 3145736 | tf_op jit(solution)/shard_map/ppermute | solution.py:16
  46.1 35.8 %collective-permute-start.2 = (bf16[1024,512]{0,1:T(8,128)(2,1)}, bf16[1024,512]{0,1:T(8,128)(2,1)}, u32[]{:S(2)}, u32[]{:S(2)}) collective-permute-start(bf16[1024,512]{0,1:T(8,128)(2,1)} %bitcast_dynamic-update-slice_fusion), channel_id=1, source_target_pairs={{0,3},{1,4},{2,5},{3,6},{4,7},{5,8},{6,9},{7,10},{8,11},{9,12},{10... | collective-permute-start | bytes 3145736 | tf_op jit(solution)/shard_map/ppermute | solution.py:16
  49.6 63.1 %collective-permute-start = (bf16[1024,512]{0,1:T(8,128)(2,1)}, bf16[1024,512]{0,1:T(8,128)(2,1)}, u32[]{:S(2)}, u32[]{:S(2)}) collective-permute-start(bf16[1024,512]{0,1:T(8,128)(2,1)} %bitcast_dynamic-update-slice_fusion), channel_id=1, source_target_pairs={{0,1},{1,2},{2,3},{3,4},{4,5},{5,6},{6,7},{7,8},{8,9},{9,10},{10,1... | collective-permute-start | bytes 3145736 | tf_op jit(solution)/shard_map/ppermute | solution.py:16
  61.4 12.9 %copy-start.2 = (bf16[1024,2,2,128]{0,3,2,1:T(8,128)(2,1)S(1)}, bf16[1024,2,2,128]{0,3,2,1:T(8,128)(2,1)}, u32[]{:S(2)}) copy-start(bf16[1024,2,2,128]{0,3,2,1:T(8,128)(2,1)} %reshape.353) | copy-start | bytes 3145732
  81.8 32.9 %copy-start = (pred[1024,1024]{0,1:T(8,128)(4,1)S(1)}, pred[1024,1024]{0,1:T(8,128)(4,1)}, u32[]{:S(2)}) copy-start(pred[1024,1024]{0,1:T(8,128)(4,1)} %get-tuple-element.36) | copy-start | bytes 3145732
  83.2 39.1 %copy-start.1 = (pred[1024,1024]{0,1:T(8,128)(4,1)S(1)}, pred[1024,1024]{0,1:T(8,128)(4,1)}, u32[]{:S(2)}) copy-start(pred[1024,1024]{0,1:T(8,128)(4,1)} %get-tuple-element.33) | copy-start | bytes 3145732
  132.6 13.7 %copy-start.4 = (bf16[1024,256]{0,1:T(8,128)(2,1)S(1)}, bf16[1024,256]{0,1:T(8,128)(2,1)}, u32[]{:S(2)}) copy-start(bf16[1024,256]{0,1:T(8,128)(2,1)} %get-tuple-element.22) | copy-start | bytes 1572868
  146.3 10.1 %copy-start.3 = (bf16[1024,256]{0,1:T(8,128)(2,1)S(1)}, bf16[1024,256]{0,1:T(8,128)(2,1)}, u32[]{:S(2)}) copy-start(bf16[1024,256]{0,1:T(8,128)(2,1)} %get-tuple-element.25) | copy-start | bytes 1572868
